TPU v7x, 128 devices: a whole 4x4x4 slice. The times are simulated.
128 devices in a mesh: dp: 16 (over x, y), expert: 8 (over z, core).
Axes of the slice: x: 4, y: 4, z: 4, core: 2. Of those that a mesh axis runs over, the one named last changes fastest.
Arguments:
- tokens: bfloat16 [2048, 4096], P('dp', 'expert'), may hold values from -6 to 6
- output_gradient: bfloat16 [2048, 4096], P('dp', 'expert'), may hold values from -6 to 6
- routing: int32 [2048, 2], P('dp'), may hold values from 0 to 7, all different within a row; in each aligned block of 128 rows (0 to 127, 128 to 255, ...) at most 96 rows name the same one
- router_gate_values: float32 [2048, 2], P('dp'), may hold values from 0.1 to 0.9
- gate_weight: bfloat16 [8, 7168, 4096], P('expert', 'dp'), may hold values from -0.09375 to 0.09375
- up_weight: bfloat16 [8, 7168, 4096], P('expert', 'dp'), may hold values from -0.09375 to 0.09375
- down_weight: bfloat16 [8, 7168, 4096], P('expert', 'dp'), may hold values from -0.0625 to 0.0625
- adapter_lower_gate: bfloat16 [8, 16, 4096], P('expert'), may hold values from -0.09375 to 0.09375
- adapter_upper_gate: bfloat16 [8, 7168, 16], P('expert', 'dp'), may hold values from -0.375 to 0.375
- adapter_lower_up: bfloat16 [8, 16, 4096], P('expert'), may hold values from -0.09375 to 0.09375
- adapter_upper_up: bfloat16 [8, 7168, 16], P('expert', 'dp'), may hold values from -0.375 to 0.375
- adapter_lower_down: bfloat16 [8, 16, 7168], P('expert', None, 'dp'), may hold values from -0.0625 to 0.0625
- adapter_upper_down: bfloat16 [8, 4096, 16], P('expert'), may hold values from -0.375 to 0.375
Outputs:
- grad_x: bfloat16 [2048, 4096], P('dp', 'expert')
- grad_lora_a_gate: float32 [8, 16, 4096], P('expert')
- grad_lora_b_gate: float32 [8, 7168, 16], P('expert', 'dp')
- grad_lora_a_up: float32 [8, 16, 4096], P('expert')
- grad_lora_b_up: float32 [8, 7168, 16], P('expert', 'dp')
- grad_lora_a_down: float32 [8, 16, 7168], P('expert', None, 'dp')
- grad_lora_b_down: float32 [8, 4096, 16], P('expert')
Inputs may be any that keep to these rules, and one draw needn't show every extreme that they name: `routing`: each row names two different experts. In the rows of one dp shard (aligned blocks of 128 rows) no expert is named by more than 96 rows, and in some blocks one expert is named by exactly 96 rows.
All inputs are finite; a program needn't handle non-finite values.
Results may differ from a plain program's by a relative error of at most 0.015.
Values may be sent and summed in bfloat16 or wider, within the bound.
A program may use at most 256 MiB of HBM per device.

v0:
```python
import jax
import jax.numpy as jnp
from jax import lax
from jax.sharding import PartitionSpec as P

ADAPTER_SCALE = 2.0


def contract_pair(left, right, left_axis, right_axis):
    return lax.dot_general(
        left, right, (((left_axis,), (right_axis,)), ((), ())), preferred_element_type=jnp.float32
    )


def slot_numbers(route_rows, experts):
    picked = (route_rows[:, :, None] == jnp.arange(experts, dtype=jnp.int32)[None, None, :]).astype(
        jnp.int32
    )
    per_token = jnp.sum(picked, axis=1)
    earlier = jnp.cumsum(per_token, axis=0) - per_token
    return jnp.sum(earlier[:, None, :] * picked, axis=2)


def slot_sources(route_rows, positions, experts, capacity):
    tokens_here, choose = route_rows.shape
    target = (route_rows * capacity + positions).reshape(-1)
    owners = jnp.repeat(jnp.arange(tokens_here, dtype=jnp.int32), choose)
    member_ids = jnp.tile(jnp.arange(choose, dtype=jnp.int32), tokens_here)
    source = jnp.full((experts * capacity,), tokens_here, jnp.int32).at[target].set(owners)
    member = jnp.zeros((experts * capacity,), jnp.int32).at[target].set(member_ids)
    return (source, member)


def rows_backward_pass(input_rows, output_gradient_rows, params):
    (
        gate_weight,
        up_weight,
        down_weight,
        a_gate,
        gate_adapter_upper,
        a_up,
        up_adapter_upper,
        down_adapter_lower,
        b_down,
    ) = params
    gate_projected_lower = contract_pair(a_gate, input_rows, 1, 1).astype(jnp.bfloat16)
    up_projected_lower = contract_pair(a_up, input_rows, 1, 1).astype(jnp.bfloat16)
    gate_preactivation = contract_pair(
        gate_weight, input_rows, 1, 1
    ) + ADAPTER_SCALE * contract_pair(gate_adapter_upper, gate_projected_lower, 1, 0)
    up_preactivation = contract_pair(up_weight, input_rows, 1, 1) + ADAPTER_SCALE * contract_pair(
        up_adapter_upper, up_projected_lower, 1, 0
    )
    sigmoid_gate = jax.nn.sigmoid(gate_preactivation)
    silu_gate = gate_preactivation * sigmoid_gate
    hidden_units = (silu_gate * up_preactivation).astype(jnp.bfloat16)
    down_projected_lower = contract_pair(b_down, output_gradient_rows, 0, 1).astype(jnp.bfloat16)
    hidden_gradient = contract_pair(
        down_weight, output_gradient_rows, 1, 1
    ) + ADAPTER_SCALE * contract_pair(down_adapter_lower, down_projected_lower, 0, 0)
    gate_gradient = (
        hidden_gradient
        * up_preactivation
        * sigmoid_gate
        * (1.0 + gate_preactivation * (1.0 - sigmoid_gate))
    ).astype(jnp.bfloat16)
    up_gradient = (hidden_gradient * silu_gate).astype(jnp.bfloat16)
    gate_partial = contract_pair(gate_adapter_upper, gate_gradient, 0, 0).astype(jnp.bfloat16)
    up_partial = contract_pair(up_adapter_upper, up_gradient, 0, 0).astype(jnp.bfloat16)
    down_partial = contract_pair(down_adapter_lower, hidden_units, 1, 0).astype(jnp.bfloat16)
    paired_partials = jnp.concatenate([gate_partial, up_partial], 0)
    paired_factors = jnp.concatenate([a_gate, a_up], 0)
    gradient_rows_out = (
        contract_pair(gate_gradient, gate_weight, 0, 0)
        + contract_pair(up_gradient, up_weight, 0, 0)
        + ADAPTER_SCALE * contract_pair(paired_partials, paired_factors, 0, 0)
    )
    shared_slice = (
        ADAPTER_SCALE * contract_pair(gate_partial, input_rows, 1, 0),
        ADAPTER_SCALE * contract_pair(up_partial, input_rows, 1, 0),
        ADAPTER_SCALE * contract_pair(output_gradient_rows, down_partial, 0, 1),
    )
    owned_slice = (
        ADAPTER_SCALE * contract_pair(gate_gradient, gate_projected_lower, 1, 1),
        ADAPTER_SCALE * contract_pair(up_gradient, up_projected_lower, 1, 1),
        ADAPTER_SCALE * contract_pair(down_projected_lower, hidden_units, 1, 1),
    )
    return (gradient_rows_out, shared_slice, owned_slice)


def local(
    tokens,
    output_gradient,
    routing,
    router_gate_values,
    gate_weight,
    up_weight,
    down_weight,
    adapter_lower_gate,
    adapter_upper_gate,
    adapter_lower_up,
    adapter_upper_up,
    adapter_lower_down,
    adapter_upper_down,
):
    experts = lax.axis_size("expert")
    shards = lax.axis_size("dp")
    tok_local, feat_local = tokens.shape
    choose = routing.shape[1]
    complete_width = feat_local * experts
    capacity = min(tok_local, 6 * tok_local // experts)
    hidden_units_local = gate_weight.shape[1]
    adapter_rank = adapter_lower_gate.shape[1]
    params = (
        gate_weight[0],
        up_weight[0],
        down_weight[0],
        adapter_lower_gate[0],
        adapter_upper_gate[0],
        adapter_lower_up[0],
        adapter_upper_up[0],
        adapter_lower_down[0],
        adapter_upper_down[0],
    )
    positions = slot_numbers(routing, experts)
    zero_row = jnp.zeros((1, feat_local), jnp.bfloat16)
    initial = (
        jnp.zeros((shards * capacity, complete_width), jnp.float32),
        (
            jnp.zeros((adapter_rank, complete_width), jnp.float32),
            jnp.zeros((adapter_rank, complete_width), jnp.float32),
            jnp.zeros((complete_width, adapter_rank), jnp.float32),
        ),
        (
            jnp.zeros((hidden_units_local, adapter_rank), jnp.float32),
            jnp.zeros((hidden_units_local, adapter_rank), jnp.float32),
            jnp.zeros((adapter_rank, hidden_units_local), jnp.float32),
        ),
    )
    source, member = slot_sources(routing, positions, experts, capacity)
    clamped = jnp.minimum(source, tok_local - 1)
    slot_gate = jnp.where(
        source < tok_local, router_gate_values.reshape(-1)[clamped * choose + member], 0.0
    )
    send_x = jnp.concatenate([tokens, zero_row], 0)[source].reshape(experts, capacity, feat_local)
    send_dy = (
        (
            slot_gate[:, None]
            * jnp.concatenate([output_gradient, zero_row], 0)[source].astype(jnp.float32)
        )
        .astype(jnp.bfloat16)
        .reshape(experts, capacity, feat_local)
    )
    recv_x, recv_dy = (
        lax.all_to_all(send_x, "expert", split_axis=0, concat_axis=2, tiled=True),
        lax.all_to_all(send_dy, "expert", split_axis=0, concat_axis=2, tiled=True),
    )
    gradient_rows_out, shared_slice, owned_slice = rows_backward_pass(
        lax.all_gather(recv_x[0], "dp", axis=0, tiled=True),
        lax.all_gather(recv_dy[0], "dp", axis=0, tiled=True),
        params,
    )
    rows_part = gradient_rows_out
    totals = (
        rows_part,
        jax.tree.map(jnp.add, initial[1], shared_slice),
        jax.tree.map(jnp.add, initial[2], owned_slice),
    )
    rows_part, shared_slice, owned_slice = totals
    summed = lax.psum_scatter(
        rows_part.astype(jnp.bfloat16), "dp", scatter_dimension=0, tiled=True
    ).astype(jnp.float32)
    returned_rows = lax.all_to_all(
        summed.reshape(capacity, experts, feat_local).astype(jnp.bfloat16),
        "expert",
        split_axis=1,
        concat_axis=1,
        tiled=True,
    ).astype(jnp.float32)
    lookup = positions * experts + routing
    grad_x = jnp.sum(returned_rows.reshape(capacity * experts, feat_local)[lookup], axis=1).astype(
        jnp.bfloat16
    )
    grad_a_gate, grad_a_up, grad_b_down = (
        lax.psum(shared_slice[0].astype(jnp.bfloat16), "dp").astype(jnp.float32),
        lax.psum(shared_slice[1].astype(jnp.bfloat16), "dp").astype(jnp.float32),
        lax.psum(shared_slice[2].astype(jnp.bfloat16), "dp").astype(jnp.float32),
    )
    return (
        grad_x,
        grad_a_gate[None],
        owned_slice[0][None],
        grad_a_up[None],
        owned_slice[1][None],
        owned_slice[2][None],
        grad_b_down[None],
    )


def solution(mesh):
    return jax.shard_map(
        local,
        mesh=mesh,
        in_specs=(
            P("dp", "expert"),
            P("dp", "expert"),
            P("dp", None),
            P("dp", None),
            P("expert", "dp", None),
            P("expert", "dp", None),
            P("expert", "dp", None),
            P("expert", None, None),
            P("expert", "dp", None),
            P("expert", None, None),
            P("expert", "dp", None),
            P("expert", None, "dp"),
            P("expert", None, None),
        ),
        out_specs=(
            P("dp", "expert"),
            P("expert", None, None),
            P("expert", "dp", None),
            P("expert", None, None),
            P("expert", "dp", None),
            P("expert", None, "dp"),
            P("expert", None, None),
        ),
        check_vma=False,
    )
```

profile of v0, /device:TPU:0, one launch (start us, length us, event | category | flops | bytes accessed | tf_op | source)
XLA Modules:
  0.0 502.2 jit_solution(6191401442853904213)
XLA Ops:
  14.0 2.7 gather_fusion.2
  16.7 18.4 %all_to_all.35 = bf16[8,96,512]{2,1,0:T(8,128)(2,1)S(1)} all-to-all(bf16[8,96,512]{2,1,0:T(8,128)(2,1)S(1)} %bitcast.118), channel_id=1, replica_groups=mesh['dp'=16,'expert'=8] {'expert'}, dimensions={0} | all-to-all | bytes 1572864 | tf_op jit(solution)/shard_map/all_to_all | solution.py:155
  36.5 5.0 gather_fusion
  41.6 2.7 gather_fusion.1
  44.5 15.7 %all_to_all.36 = bf16[8,96,512]{2,1,0:T(8,128)(2,1)S(1)} all-to-all(bf16[8,96,512]{2,1,0:T(8,128)(2,1)S(1)} %fusion.23), channel_id=1, replica_groups=mesh['dp'=16,'expert'=8] {'expert'}, dimensions={0} | all-to-all | bytes 1572864 | tf_op jit(solution)/shard_map/all_to_all | solution.py:156
  61.8 63.9 %all-gather.5.cloned.1.call-done = bf16[1536,4096]{1,0:T(8,128)(2,1)} async-done(((bf16[96,4096]{1,0:T(8,128)(2,1)}), bf16[1536,4096]{1,0:T(8,128)(2,1)}) %all-gather.5.cloned.1.call-update) | async-done | bytes 12582928 | tf_op jit(solution)/shard_map/all_gather | solution.py:159
  125.7 8.1 %convolution_convert_fusion.3 = bf16[1536,16]{0,1:T(8,128)(2,1)S(1)} fusion(bf16[1536,4096]{1,0:T(8,128)(2,1)} %all-gather.5.cloned.1.call-done, bf16[1,16,4096]{2,1,0:T(8,128)(2,1)S(1)} %copy-done.5), kind=kOutput, calls=%fused_computation.43 | convolution fusion | flops 201351168 | bytes 12763136 | tf_op jit(solution)/shard_map/dot_general | solution.py:10
  133.9 8.0 %fusion.8 = f32[1536,448]{0,1:T(8,128)S(1)} fusion(bf16[1536,4096]{1,0:T(8,128)(2,1)S(1)} %copy-done.2, bf16[1,448,4096]{2,1,0:T(8,128)(2,1)} %param.17), kind=kOutput, calls=%fused_computation.18 | convolution fusion | flops 5637144576 | bytes 19005440 | tf_op jit(solution)/shard_map/dot_general | solution.py:10
  141.8 2.1 fusion.21
  144.0 73.6 %all-gather.3.cloned.1.call-done = bf16[1536,4096]{1,0:T(8,128)(2,1)} async-done(((bf16[96,4096]{1,0:T(8,128)(2,1)}), bf16[1536,4096]{1,0:T(8,128)(2,1)}) %all-gather.3.cloned.1.call-update) | async-done | bytes 12582928 | tf_op jit(solution)/shard_map/all_gather | solution.py:160
  217.5 8.1 %convolution_convert_fusion.5 = bf16[1536,16]{0,1:T(8,128)(2,1)S(1)} fusion(bf16[1536,4096]{1,0:T(8,128)(2,1)} %all-gather.3.cloned.1.call-done, bf16[1,4096,16]{1,2,0:T(8,128)(2,1)S(1)} %copy-done), kind=kOutput, calls=%fused_computation.45 | convolution fusion | flops 201351168 | bytes 12763136 | tf_op jit(solution)/shard_map/dot_general | solution.py:10
  225.6 9.3 %fusion.14 = f32[1536,448]{0,1:T(8,128)S(1)} fusion(bf16[1536,4096]{1,0:T(8,128)(2,1)} %all-gather.3.cloned.1.call-done, bf16[1,448,4096]{2,1,0:T(8,128)(2,1)S(1)} %copy-done.12), kind=kOutput, calls=%fused_computation.24 | convolution fusion | flops 5637144576 | bytes 19005440 | tf_op jit(solution)/shard_map/dot_general | solution.py:10
  235.8 3.3 convolution_convert_fusion.4
  239.2 5.9 %fusion.12 = f32[1536,448]{0,1:T(8,128)S(1)} fusion(bf16[1536,4096]{1,0:T(8,128)(2,1)S(1)} %bitcast.115, bf16[1,448,4096]{2,1,0:T(8,128)(2,1)S(1)} %copy-done.13), kind=kOutput, calls=%fused_computation.22 | convolution fusion | flops 5637144576 | bytes 19005440 | tf_op jit(solution)/shard_map/dot_general | solution.py:10
  245.1 2.7 multiply_convert_fusion
  248.1 12.0 %fusion.10 = f32[1536,4096]{1,0:T(8,128)} fusion(bf16[448,1536]{1,0:T(8,128)(2,1)S(1)} %get-tuple-element.12, bf16[1,448,4096]{2,1,0:T(8,128)(2,1)S(1)} %copy-done.13), kind=kOutput, calls=%fused_computation.20 | convolution fusion | flops 5637144576 | bytes 30212096 | tf_op jit(solution)/shard_map/dot_general | solution.py:10
  260.4 11.7 %fusion.6 = f32[1536,4096]{1,0:T(8,128)} fusion(bf16[448,1536]{1,0:T(8,128)(2,1)S(1)} %get-tuple-element.11, bf16[1,448,4096]{2,1,0:T(8,128)(2,1)S(1)} %copy-done.14), kind=kOutput, calls=%fused_computation.16 | convolution fusion | flops 5637144576 | bytes 30212096 | tf_op jit(solution)/shard_map/dot_general | solution.py:10
  272.1 21.9 %add_convert_fusion = bf16[1536,4096]{1,0:T(8,128)(2,1)} fusion(f32[1536,4096]{1,0:T(8,128)} %fusion.6, f32[1536,4096]{1,0:T(8,128)} %fusion.10, bf16[16,4096]{1,0:T(8,128)(2,1)S(1)} %bitcast.128, bf16[16,4096]{1,0:T(8,128)(2,1)S(1)} %bitcast.127, bf16[16,1536]{1,0:T(8,128)(2,1)S(1)} %bitcast.126, bf16[16,1536]{1,0:T(8,128)(2,1)S(1)} %bitcast.125), kind=kOutput, calls=%fused_computation.6 | convolution fusion | flops 428539904 | bytes 63275008 | tf_op jit(solution)/shard_map/dot_general | solution.py:10
  294.3 7.0 %fusion.4 = bf16[1,16,4096]{2,1,0:T(8,128)(2,1)} fusion(bf16[1536,16]{0,1:T(8,128)(2,1)S(1)} %convolution_convert_fusion.1, bf16[1536,4096]{1,0:T(8,128)(2,1)} %all-gather.5.cloned.1.call-done), kind=kOutput, calls=%fused_computation.14 | convolution fusion | flops 201457664 | bytes 12763136 | tf_op jit(solution)/shard_map/dot_general | solution.py:10
  301.2 8.2 %fusion.3 = bf16[1,4096,16]{1,2,0:T(8,128)(2,1)} fusion(bf16[1536,4096]{1,0:T(8,128)(2,1)} %all-gather.3.cloned.1.call-done, bf16[448,1536]{1,0:T(8,128)(2,1)} %get-tuple-element.10, bf16[1,16,448]{2,1,0:T(8,128)(2,1)S(1)} %copy-done.9), kind=kOutput, calls=%fused_computation.13 | convolution fusion | flops 223502336 | bytes 14104576 | tf_op jit(solution)/shard_map/dot_general | solution.py:10
  309.4 78.8 %reduce-scatter.2.cloned.1.call-done = bf16[96,4096]{1,0:T(8,128)(2,1)} async-done(((bf16[1536,4096]{1,0:T(8,128)(2,1)}), bf16[96,4096]{1,0:T(8,128)(2,1)}) %reduce-scatter.2.cloned.1.call-update) | async-done | bytes 786448 | tf_op jit(solution)/shard_map/reduce_scatter | solution.py:170
  390.4 4.4 all-to-all-start.2
  395.1 7.0 %fusion.5 = bf16[1,16,4096]{2,1,0:T(8,128)(2,1)} fusion(bf16[1536,16]{0,1:T(8,128)(2,1)S(1)} %convolution_convert_fusion.2, bf16[1536,4096]{1,0:T(8,128)(2,1)} %all-gather.5.cloned.1.call-done), kind=kOutput, calls=%fused_computation.15 | convolution fusion | flops 201457664 | bytes 12763136 | tf_op jit(solution)/shard_map/dot_general | solution.py:10
  405.4 80.9 %all-reduce.5.cloned.1.call-done = (bf16[1,16,4096]{2,1,0:T(8,128)(2,1)}, bf16[1,16,4096]{2,1,0:T(8,128)(2,1)}, bf16[1,4096,16]{1,2,0:T(8,128)(2,1)}) async-done(((bf16[1,16,4096]{2,1,0:T(8,128)(2,1)}, bf16[1,16,4096]{2,1,0:T(8,128)(2,1)}, bf16[1,4096,16]{1,2,0:T(8,128)(2,1)}), (bf16[1,16,4096]{2,1,0:T(8,128)(2,1)}, bf16[1,16,4096]{2,1,0:T(8,128)(2,1)}, ...) | async-done | bytes 393232 | tf_op jit(solution)/shard_map/psum | solution.py:185
  (90 shorter events, 26.6 us)
Async XLA Ops:
  7.2 210.4 %copy-start = (bf16[1,4096,16]{1,2,0:T(8,128)(2,1)S(1)}, bf16[1,4096,16]{1,2,0:T(8,128)(2,1)}, u32[]{:S(2)}) copy-start(bf16[1,4096,16]{1,2,0:T(8,128)(2,1)} %param.25) | copy-start | bytes 393220
  7.2 118.5 %all-gather.5.cloned.1.call-start = ((), (), s32[]{:S(2)}) async-start(), calls=%async_computation.5 | async-start | bytes 13369344 | tf_op jit(solution)/shard_map/all_gather | solution.py:159
  16.7 19.5 %copy-start.11 = (f32[128,2]{0,1:T(2,128)S(1)}, f32[128,2]{0,1:T(2,128)}, u32[]{:S(2)}) copy-start(f32[128,2]{0,1:T(2,128)} %param.16) | copy-start | bytes 3076
  36.1 5.4 %copy-start.7 = (bf16[128,512]{1,0:T(8,128)(2,1)S(1)}, bf16[128,512]{1,0:T(8,128)(2,1)}, u32[]{:S(2)}) copy-start(bf16[128,512]{1,0:T(8,128)(2,1)} %param.14) | copy-start | bytes 393220
  36.2 181.3 %all-gather.3.cloned.1.call-start = ((), (), s32[]{:S(2)}) async-start(), calls=%async_computation.4 | async-start | bytes 13369344 | tf_op jit(solution)/shard_map/all_gather | solution.py:160
  44.3 81.4 %copy-start.5 = (bf16[1,16,4096]{2,1,0:T(8,128)(2,1)S(1)}, bf16[1,16,4096]{2,1,0:T(8,128)(2,1)}, u32[]{:S(2)}) copy-start(bf16[1,16,4096]{2,1,0:T(8,128)(2,1)} %param.20) | copy-start | bytes 393220
  61.2 327.1 %reduce-scatter.2.cloned.1.call-start = ((), (), s32[]{:S(2)}) async-start(), calls=%async_computation.6 | async-start | bytes 13369344 | tf_op jit(solution)/shard_map/reduce_scatter | solution.py:170
  125.7 8.2 %copy-start.2 = (bf16[1536,4096]{1,0:T(8,128)(2,1)S(1)}, bf16[1536,4096]{1,0:T(8,128)(2,1)}, u32[]{:S(2)}) copy-start(bf16[1536,4096]{1,0:T(8,128)(2,1)} %all-gather.5.cloned.1.call-done) | copy-start | bytes 37748740
  133.9 8.0 %copy-start.8 = (bf16[1,448,16]{1,2,0:T(8,128)(2,1)S(1)}, bf16[1,448,16]{1,2,0:T(8,128)(2,1)}, u32[]{:S(2)}) copy-start(bf16[1,448,16]{1,2,0:T(8,128)(2,1)} %param.21) | copy-start | bytes 43012
  217.5 8.1 %copy-start.12 = (bf16[1,448,4096]{2,1,0:T(8,128)(2,1)S(1)}, bf16[1,448,4096]{2,1,0:T(8,128)(2,1)}, u32[]{:S(2)}) copy-start(bf16[1,448,4096]{2,1,0:T(8,128)(2,1)} %param.19) | copy-start | bytes 11010052
  217.5 18.0 %slice-start = ((s8[12582912]{0:T(1024)(128)(4,1)}), s8[4194304]{0:T(1024)(128)(4,1)S(1)}, s32[]{:S(2)}) async-start(s8[12582912]{0:T(1024)(128)(4,1)} %bitcast.114), calls=%async_computation.8 | async-start | bytes 8388608
  225.6 9.3 %copy-start.9 = (bf16[1,16,448]{2,1,0:T(8,128)(2,1)S(1)}, bf16[1,16,448]{2,1,0:T(8,128)(2,1)}, u32[]{:S(2)}) copy-start(bf16[1,16,448]{2,1,0:T(8,128)(2,1)} %param.24) | copy-start | bytes 43012
  225.6 9.9 %slice-start.1 = ((s8[12582912]{0:T(1024)(128)(4,1)}), s8[4194304]{0:T(1024)(128)(4,1)S(1)}, s32[]{:S(2)}) async-start(s8[12582912]{0:T(1024)(128)(4,1)} %bitcast.114), calls=%async_computation.9 | async-start | bytes 8388608
  225.6 9.9 %slice-start.2 = ((s8[12582912]{0:T(1024)(128)(4,1)}), s8[4194304]{0:T(1024)(128)(4,1)S(1)}, s32[]{:S(2)}) async-start(s8[12582912]{0:T(1024)(128)(4,1)} %bitcast.114), calls=%async_computation.10 | async-start | bytes 8388608
  234.9 0.9 copy-start.6
  235.8 3.3 copy-start.13
  239.2 5.9 %copy-start.4 = (f32[448,1536]{1,0:T(8,128)S(1)}, f32[448,1536]{1,0:T(8,128)}, u32[]{:S(2)}) copy-start(f32[448,1536]{1,0:T(8,128)} %fusion.21) | copy-start | bytes 8257540
  239.2 5.9 %copy-start.10 = (bf16[1,448,16]{1,2,0:T(8,128)(2,1)S(1)}, bf16[1,448,16]{1,2,0:T(8,128)(2,1)}, u32[]{:S(2)}) copy-start(bf16[1,448,16]{1,2,0:T(8,128)(2,1)} %param.23) | copy-start | bytes 43012
  248.1 12.2 %copy-start.14 = (bf16[1,448,4096]{2,1,0:T(8,128)(2,1)S(1)}, bf16[1,448,4096]{2,1,0:T(8,128)(2,1)}, u32[]{:S(2)}) copy-start(bf16[1,448,4096]{2,1,0:T(8,128)(2,1)} %param.17) | copy-start | bytes 11010052
  390.4 100.9 %all-to-all-start.2 = ((bf16[96,8,512]{2,0,1:T(8,128)(2,1)}), bf16[96,8,512]{2,0,1:T(8,128)(2,1)}, u32[]{:S(2)}, u32[]{:S(2)}) async-start(bf16[96,8,512]{2,0,1:T(8,128)(2,1)} %bitcast.119), calls=%async_computation.3 | async-start | bytes 1572864 | tf_op jit(solution)/shard_map/all_to_all | solution.py:173
  394.8 91.6 %all-reduce.5.cloned.1.call-start = ((), (), s32[]{:S(2)}) async-start(), calls=%async_computation.7 | async-start | bytes 786432 | tf_op jit(solution)/shard_map/psum | solution.py:185
  402.1 2.2 copy-start.3
  492.8 2.6 copy-start.1
Sparse Core Ops, SparseCore 0:
  36.3 89.3 all-gather.4
  127.9 89.5 all-gather.2
  294.1 94.1 reduce-scatter.1
  402.2 84.0 all-reduce.4
where the time goes:
time: 507 us; the launch traced here: 502 us
  waiting for transfers between devices  297 us (59%)
  matrix products  120 us (24%)
  blocking collectives  34.1 us (7%)
  local copies, waits for them, and re-layouts  22.7 us (4%)
  between operations  14.4 us (3%)
  other arithmetic  8.74 us (2%)
  starting transfers between devices  5.36 us (1%)
    dot_general x20, matrix products, contract_pair(): lax.dot_general(left, right, (((left_axis,), (right_axis,)), ((), ())), p...  120 us
    psum x1, waiting for transfers between devices, local(): lax.psum(shared_slice[0].astype(jnp.bfloat16), 'dp').astype(jnp.float32)  80.9 us
    reduce_scatter x1, waiting for transfers between devices, local(): lax.psum_scatter(rows_part.astype(jnp.bfloat16), 'dp', scatter_dimension=...  78.8 us
    all_gather x1, waiting for transfers between devices, local(): lax.all_gather(recv_dy[0], 'dp', axis=0, tiled=True)  73.6 us
    all_gather x1, waiting for transfers between devices, local(): lax.all_gather(recv_x[0], 'dp', axis=0, tiled=True)  63.9 us
    all_to_all x1, blocking collectives, local(): lax.all_to_all(send_x, 'expert', split_axis=0, concat_axis=2, tiled=True)  18.4 us
    all_to_all x1, blocking collectives, local(): lax.all_to_all(send_dy, 'expert', split_axis=0, concat_axis=2, tiled=True)  15.7 us
  transfers between devices with their start and end apart: 5, of which 4 were waited for; matrix products, arithmetic and copies ran while one was open for 12% of the time, Pallas kernels for 0%

commit v1 on v0

--- a/solution.py
+++ b/solution.py
@@ -182,7 +182,9 @@
         jnp.bfloat16
     )
     grad_a_gate, grad_a_up, grad_b_down = (
-        lax.psum(shared_slice[0].astype(jnp.bfloat16), "dp").astype(jnp.float32),
+        jnp.sum(lax.all_gather(shared_slice[0].astype(jnp.bfloat16), "dp"), axis=0).astype(
+            jnp.float32
+        ),
         lax.psum(shared_slice[1].astype(jnp.bfloat16), "dp").astype(jnp.float32),
         lax.psum(shared_slice[2].astype(jnp.bfloat16), "dp").astype(jnp.float32),
     )

time: 507 us -> 539 us (1.063)
  waiting for transfers between devices: 297 us -> 327 us
    all_gather x0 -> x1, waiting for transfers between devices: none -> 43.8 us  [local(): lax.all_gather(shared_slice[0].astype(jnp.bfloat16), 'dp')]
    psum x1, waiting for transfers between devices: 80.9 us -> 37.3 us  [local(): lax.psum(shared_slice[1].astype(jnp.bfloat16), 'dp').astype(jnp.float32)]
    reduce_scatter x1, waiting for transfers between devices: 78.8 us -> 95.5 us  [local(): lax.psum_scatter(rows_part.astype(jnp.bfloat16), 'dp', scatter_dimension=...]
    all_to_all x1, waiting for transfers between devices: 0.01 us -> 12.4 us  [local(): lax.all_to_all(summed.reshape(capacity, experts, feat_local).astype(jnp.b...]
  transfers between devices with their start and end apart: 5 -> 6, of which waited for: 4 -> 6; matrix products, arithmetic and copies ran while one was open for 12% -> 15% of each run, Pallas kernels for 0% -> 0%
where the time goes in v1:
time: 539 us; the launch traced here: 533 us
  waiting for transfers between devices  327 us (61%)
  matrix products  122 us (23%)
  blocking collectives  34.1 us (6%)
  local copies, waits for them, and re-layouts  21.6 us (4%)
  between operations  14.3 us (3%)
  other arithmetic  9.74 us (2%)
    dot_general x20, matrix products, contract_pair(): lax.dot_general(left, right, (((left_axis,), (right_axis,)), ((), ())), p...  122 us
    reduce_scatter x1, waiting for transfers between devices, local(): lax.psum_scatter(rows_part.astype(jnp.bfloat16), 'dp', scatter_dimension=...  95.5 us
    all_gather x1, waiting for transfers between devices, local(): lax.all_gather(recv_dy[0], 'dp', axis=0, tiled=True)  73.6 us
    all_gather x1, waiting for transfers between devices, local(): lax.all_gather(recv_x[0], 'dp', axis=0, tiled=True)  64.2 us
    all_gather x1, waiting for transfers between devices, local(): lax.all_gather(shared_slice[0].astype(jnp.bfloat16), 'dp')  43.8 us
    psum x1, waiting for transfers between devices, local(): lax.psum(shared_slice[1].astype(jnp.bfloat16), 'dp').astype(jnp.float32)  37.3 us
    all_to_all x1, blocking collectives, local(): lax.all_to_all(send_x, 'expert', split_axis=0, concat_axis=2, tiled=True)  18.4 us
    all_to_all x1, blocking collectives, local(): lax.all_to_all(send_dy, 'expert', split_axis=0, concat_axis=2, tiled=True)  15.7 us
  transfers between devices with their start and end apart: 6, of which 6 were waited for; matrix products, arithmetic and copies ran while one was open for 15% of the time, Pallas kernels for 0%

profile of v1, /device:TPU:0, one launch (start us, length us, event | category | flops | bytes accessed | tf_op | source)
XLA Modules:
  0.0 533.2 jit_solution(13650399925861427518)
XLA Ops:
  14.0 2.7 gather_fusion.2
  16.7 18.4 %all_to_all.35 = bf16[8,96,512]{2,1,0:T(8,128)(2,1)S(1)} all-to-all(bf16[8,96,512]{2,1,0:T(8,128)(2,1)S(1)} %bitcast.120), channel_id=1, replica_groups=mesh['dp'=16,'expert'=8] {'expert'}, dimensions={0} | all-to-all | bytes 1572864 | tf_op jit(solution)/shard_map/all_to_all | solution.py:155
  36.5 5.0 gather_fusion
  44.5 15.7 %all_to_all.36 = bf16[8,96,512]{2,1,0:T(8,128)(2,1)S(1)} all-to-all(bf16[8,96,512]{2,1,0:T(8,128)(2,1)S(1)} %fusion.22), channel_id=1, replica_groups=mesh['dp'=16,'expert'=8] {'expert'}, dimensions={0} | all-to-all | bytes 1572864 | tf_op jit(solution)/shard_map/all_to_all | solution.py:156
  61.5 64.2 %all-gather.7.cloned.1.call-done = bf16[1536,4096]{1,0:T(8,128)(2,1)} async-done(((bf16[96,4096]{1,0:T(8,128)(2,1)}), bf16[1536,4096]{1,0:T(8,128)(2,1)}) %all-gather.7.cloned.1.call-update) | async-done | bytes 12582928 | tf_op jit(solution)/shard_map/all_gather | solution.py:159
  125.7 8.1 %convolution_convert_fusion.3 = bf16[1536,16]{0,1:T(8,128)(2,1)S(1)} fusion(bf16[1536,4096]{1,0:T(8,128)(2,1)} %all-gather.7.cloned.1.call-done, bf16[1,16,4096]{2,1,0:T(8,128)(2,1)S(1)} %copy-done.5), kind=kOutput, calls=%fused_computation.42 | convolution fusion | flops 201351168 | bytes 12763136 | tf_op jit(solution)/shard_map/dot_general | solution.py:10
  133.9 8.0 %fusion.7 = f32[1536,448]{0,1:T(8,128)S(1)} fusion(bf16[1536,4096]{1,0:T(8,128)(2,1)S(1)} %copy-done.2, bf16[1,448,4096]{2,1,0:T(8,128)(2,1)} %param.17), kind=kOutput, calls=%fused_computation.17 | convolution fusion | flops 5637144576 | bytes 19005440 | tf_op jit(solution)/shard_map/dot_general | solution.py:10
  144.0 73.6 %all-gather.5.cloned.1.call-done = bf16[1536,4096]{1,0:T(8,128)(2,1)} async-done(((bf16[96,4096]{1,0:T(8,128)(2,1)}), bf16[1536,4096]{1,0:T(8,128)(2,1)}) %all-gather.5.cloned.1.call-update) | async-done | bytes 12582928 | tf_op jit(solution)/shard_map/all_gather | solution.py:160
  217.5 8.1 %convolution_convert_fusion.5 = bf16[1536,16]{0,1:T(8,128)(2,1)S(1)} fusion(bf16[1536,4096]{1,0:T(8,128)(2,1)} %all-gather.5.cloned.1.call-done, bf16[1,4096,16]{1,2,0:T(8,128)(2,1)S(1)} %copy-done), kind=kOutput, calls=%fused_computation.44 | convolution fusion | flops 201351168 | bytes 12763136 | tf_op jit(solution)/shard_map/dot_general | solution.py:10
  225.6 9.5 %fusion.13 = f32[1536,448]{0,1:T(8,128)S(1)} fusion(bf16[1536,4096]{1,0:T(8,128)(2,1)} %all-gather.5.cloned.1.call-done, bf16[1,448,4096]{2,1,0:T(8,128)(2,1)S(1)} %copy-done.12), kind=kOutput, calls=%fused_computation.23 | convolution fusion | flops 5637144576 | bytes 19005440 | tf_op jit(solution)/shard_map/dot_general | solution.py:10
  236.1 3.3 convolution_convert_fusion.4
  239.5 5.9 %fusion.11 = f32[1536,448]{0,1:T(8,128)S(1)} fusion(bf16[1536,4096]{1,0:T(8,128)(2,1)S(1)} %bitcast.117, bf16[1,448,4096]{2,1,0:T(8,128)(2,1)S(1)} %copy-done.13), kind=kOutput, calls=%fused_computation.21 | convolution fusion | flops 5637144576 | bytes 19005440 | tf_op jit(solution)/shard_map/dot_general | solution.py:10
  245.4 2.7 multiply_convert_fusion
  248.4 12.0 %fusion.9 = f32[1536,4096]{1,0:T(8,128)} fusion(bf16[448,1536]{1,0:T(8,128)(2,1)S(1)} %get-tuple-element.11, bf16[1,448,4096]{2,1,0:T(8,128)(2,1)S(1)} %copy-done.13), kind=kOutput, calls=%fused_computation.19 | convolution fusion | flops 5637144576 | bytes 30212096 | tf_op jit(solution)/shard_map/dot_general | solution.py:10
  260.6 7.6 %fusion.3 = bf16[1,4096,16]{1,2,0:T(8,128)(2,1)} fusion(bf16[1536,4096]{1,0:T(8,128)(2,1)} %all-gather.5.cloned.1.call-done, bf16[448,1536]{1,0:T(8,128)(2,1)} %get-tuple-element.9, bf16[1,16,448]{2,1,0:T(8,128)(2,1)S(1)} %copy-done.9), kind=kOutput, calls=%fused_computation.13 | convolution fusion | flops 223502336 | bytes 14104576 | tf_op jit(solution)/shard_map/dot_general | solution.py:10
  268.2 7.0 %fusion.4 = bf16[1,16,4096]{2,1,0:T(8,128)(2,1)} fusion(bf16[1536,16]{0,1:T(8,128)(2,1)S(1)} %convolution_convert_fusion.1, bf16[1536,4096]{1,0:T(8,128)(2,1)} %all-gather.7.cloned.1.call-done), kind=kOutput, calls=%fused_computation.14 | convolution fusion | flops 201457664 | bytes 12763136 | tf_op jit(solution)/shard_map/dot_general | solution.py:10
  275.3 7.0 %fusion = bf16[16,4096]{1,0:T(8,128)(2,1)} fusion(bf16[1536,16]{0,1:T(8,128)(2,1)S(1)} %convolution_convert_fusion.2, bf16[1536,4096]{1,0:T(8,128)(2,1)} %all-gather.7.cloned.1.call-done), kind=kOutput, calls=%fused_computation.10 | convolution fusion | flops 201457664 | bytes 12763136 | tf_op jit(solution)/shard_map/dot_general | solution.py:10
  282.3 14.1 %fusion.5 = f32[1536,4096]{1,0:T(8,128)} fusion(bf16[448,1536]{1,0:T(8,128)(2,1)S(1)} %get-tuple-element.10, bf16[1,448,4096]{2,1,0:T(8,128)(2,1)} %param.17), kind=kOutput, calls=%fused_computation.15 | convolution fusion | flops 5637144576 | bytes 30212096 | tf_op jit(solution)/shard_map/dot_general | solution.py:10
  296.4 21.9 %add_convert_fusion = bf16[1536,4096]{1,0:T(8,128)(2,1)} fusion(f32[1536,4096]{1,0:T(8,128)} %fusion.5, f32[1536,4096]{1,0:T(8,128)} %fusion.9, bf16[16,4096]{1,0:T(8,128)(2,1)S(1)} %bitcast.130, bf16[16,4096]{1,0:T(8,128)(2,1)S(1)} %bitcast.129, bf16[16,1536]{1,0:T(8,128)(2,1)S(1)} %bitcast.127, bf16[16,1536]{1,0:T(8,128)(2,1)S(1)} %bitcast.128), kind=kOutput, calls=%fused_computation.6 | convolution fusion | flops 428539904 | bytes 63275008 | tf_op jit(solution)/shard_map/dot_general | solution.py:10
  321.9 37.3 %all-reduce.5.cloned.1.call-done = (bf16[1,16,4096]{2,1,0:T(8,128)(2,1)}, bf16[1,4096,16]{1,2,0:T(8,128)(2,1)}) async-done(((bf16[1,16,4096]{2,1,0:T(8,128)(2,1)}, bf16[1,4096,16]{1,2,0:T(8,128)(2,1)}), (bf16[1,16,4096]{2,1,0:T(8,128)(2,1)}, bf16[1,4096,16]{1,2,0:T(8,128)(2,1)})) %all-reduce.5.cloned.1.call-update) | async-done | bytes 262160 | tf_op jit(solution)/shard_map/psum | solution.py:188
  362.4 43.8 %all-gather.9.cloned.1.call-done = bf16[256,4096]{1,0:T(8,128)(2,1)} async-done(((bf16[16,4096]{1,0:T(8,128)(2,1)}), bf16[256,4096]{1,0:T(8,128)(2,1)}) %all-gather.9.cloned.1.call-update) | async-done | bytes 2097168 | tf_op jit(solution)/shard_map/all_gather | solution.py:185
  408.1 95.5 %reduce-scatter.2.cloned.1.call-done = bf16[96,4096]{1,0:T(8,128)(2,1)} async-done(((bf16[1536,4096]{1,0:T(8,128)(2,1)}), bf16[96,4096]{1,0:T(8,128)(2,1)}) %reduce-scatter.2.cloned.1.call-update) | async-done | bytes 786448 | tf_op jit(solution)/shard_map/reduce_scatter | solution.py:170
  505.8 4.4 all-to-all-start.2
  510.9 12.4 %all-to-all-done.2 = bf16[96,8,512]{2,0,1:T(8,128)(2,1)S(1)} async-done(((bf16[96,8,512]{2,0,1:T(8,128)(2,1)}), bf16[96,8,512]{2,0,1:T(8,128)(2,1)S(1)}, u32[]{:S(2)}, u32[]{:S(2)}) %all-to-all-start.2) | async-done | bytes 786464 | tf_op jit(solution)/shard_map/all_to_all | solution.py:173
  (92 shorter events, 30.8 us)
Async XLA Ops:
  7.2 210.4 %copy-start = (bf16[1,4096,16]{1,2,0:T(8,128)(2,1)S(1)}, bf16[1,4096,16]{1,2,0:T(8,128)(2,1)}, u32[]{:S(2)}) copy-start(bf16[1,4096,16]{1,2,0:T(8,128)(2,1)} %param.25) | copy-start | bytes 393220
  7.2 118.5 %all-gather.7.cloned.1.call-start = ((), (), s32[]{:S(2)}) async-start(), calls=%async_computation.5 | async-start | bytes 13369344 | tf_op jit(solution)/shard_map/all_gather | solution.py:159
  16.7 19.5 %copy-start.11 = (f32[128,2]{0,1:T(2,128)S(1)}, f32[128,2]{0,1:T(2,128)}, u32[]{:S(2)}) copy-start(f32[128,2]{0,1:T(2,128)} %param.16) | copy-start | bytes 3076
  36.2 5.4 %copy-start.7 = (bf16[128,512]{1,0:T(8,128)(2,1)S(1)}, bf16[128,512]{1,0:T(8,128)(2,1)}, u32[]{:S(2)}) copy-start(bf16[128,512]{1,0:T(8,128)(2,1)} %param.14) | copy-start | bytes 393220
  36.2 181.3 %all-gather.5.cloned.1.call-start = ((), (), s32[]{:S(2)}) async-start(), calls=%async_computation.4 | async-start | bytes 13369344 | tf_op jit(solution)/shard_map/all_gather | solution.py:160
  44.3 81.4 %copy-start.5 = (bf16[1,16,4096]{2,1,0:T(8,128)(2,1)S(1)}, bf16[1,16,4096]{2,1,0:T(8,128)(2,1)}, u32[]{:S(2)}) copy-start(bf16[1,16,4096]{2,1,0:T(8,128)(2,1)} %param.20) | copy-start | bytes 393220
  61.2 298.0 %all-reduce.5.cloned.1.call-start = ((), (), s32[]{:S(2)}) async-start(), calls=%async_computation.8 | async-start | bytes 524288 | tf_op jit(solution)/shard_map/psum | solution.py:188
  125.7 8.2 %copy-start.2 = (bf16[1536,4096]{1,0:T(8,128)(2,1)S(1)}, bf16[1536,4096]{1,0:T(8,128)(2,1)}, u32[]{:S(2)}) copy-start(bf16[1536,4096]{1,0:T(8,128)(2,1)} %all-gather.7.cloned.1.call-done) | copy-start | bytes 37748740
  133.9 8.0 %copy-start.8 = (bf16[1,448,16]{1,2,0:T(8,128)(2,1)S(1)}, bf16[1,448,16]{1,2,0:T(8,128)(2,1)}, u32[]{:S(2)}) copy-start(bf16[1,448,16]{1,2,0:T(8,128)(2,1)} %param.21) | copy-start | bytes 43012
  217.5 8.1 %copy-start.12 = (bf16[1,448,4096]{2,1,0:T(8,128)(2,1)S(1)}, bf16[1,448,4096]{2,1,0:T(8,128)(2,1)}, u32[]{:S(2)}) copy-start(bf16[1,448,4096]{2,1,0:T(8,128)(2,1)} %param.19) | copy-start | bytes 11010052
  217.5 18.2 %slice-start = ((s8[12582912]{0:T(1024)(128)(4,1)}), s8[4194304]{0:T(1024)(128)(4,1)S(1)}, s32[]{:S(2)}) async-start(s8[12582912]{0:T(1024)(128)(4,1)} %bitcast.116), calls=%async_computation.9 | async-start | bytes 8388608
  225.6 9.6 %copy-start.9 = (bf16[1,16,448]{2,1,0:T(8,128)(2,1)S(1)}, bf16[1,16,448]{2,1,0:T(8,128)(2,1)}, u32[]{:S(2)}) copy-start(bf16[1,16,448]{2,1,0:T(8,128)(2,1)} %param.24) | copy-start | bytes 43012
  225.6 10.2 %slice-start.1 = ((s8[12582912]{0:T(1024)(128)(4,1)}), s8[4194304]{0:T(1024)(128)(4,1)S(1)}, s32[]{:S(2)}) async-start(s8[12582912]{0:T(1024)(128)(4,1)} %bitcast.116), calls=%async_computation.10 | async-start | bytes 8388608
  225.6 10.2 %slice-start.2 = ((s8[12582912]{0:T(1024)(128)(4,1)}), s8[4194304]{0:T(1024)(128)(4,1)S(1)}, s32[]{:S(2)}) async-start(s8[12582912]{0:T(1024)(128)(4,1)} %bitcast.116), calls=%async_computation.11 | async-start | bytes 8388608
  235.2 0.9 copy-start.6
  236.1 3.3 copy-start.13
  239.4 5.9 %copy-start.4 = (f32[448,1536]{1,0:T(8,128)S(1)}, f32[448,1536]{1,0:T(8,128)}, u32[]{:S(2)}) copy-start(f32[448,1536]{1,0:T(8,128)} %fusion.20) | copy-start | bytes 8257540
  239.4 5.9 %copy-start.10 = (bf16[1,448,16]{1,2,0:T(8,128)(2,1)S(1)}, bf16[1,448,16]{1,2,0:T(8,128)(2,1)}, u32[]{:S(2)}) copy-start(bf16[1,448,16]{1,2,0:T(8,128)(2,1)} %param.23) | copy-start | bytes 43012
  275.2 131.0 %all-gather.9.cloned.1.call-start = ((), (), s32[]{:S(2)}) async-start(), calls=%async_computation.7 | async-start | bytes 2228224 | tf_op jit(solution)/shard_map/all_gather | solution.py:185
  282.3 221.4 %reduce-scatter.2.cloned.1.call-start = ((), (), s32[]{:S(2)}) async-start(), calls=%async_computation.6 | async-start | bytes 13369344 | tf_op jit(solution)/shard_map/reduce_scatter | solution.py:170
  318.6 2.2 copy-start.3
  505.8 17.6 %all-to-all-start.2 = ((bf16[96,8,512]{2,0,1:T(8,128)(2,1)}), bf16[96,8,512]{2,0,1:T(8,128)(2,1)S(1)}, u32[]{:S(2)}, u32[]{:S(2)}) async-start(bf16[96,8,512]{2,0,1:T(8,128)(2,1)} %bitcast.113), calls=%async_computation.3 | async-start | bytes 1572864 | tf_op jit(solution)/shard_map/all_to_all | solution.py:173
  523.8 2.6 copy-start.1
Sparse Core Ops, SparseCore 0:
  36.3 89.3 all-gather.6
  127.9 89.5 all-gather.4
  275.3 83.7 all-reduce.4
  362.0 44.2 all-gather.8
  409.9 93.7 reduce-scatter.1
